TPU v7x, 32 devices: a whole 2x2x4 slice. The times are simulated.
32 devices in a mesh: dp: 8 (over z, x), shard: 4 (over y, core).
Axes of the slice: x: 2, y: 2, z: 4, core: 2. Of those that a mesh axis runs over, the one named last changes fastest.
Arguments:
- noisy: float32 [128, 256, 16], P(('dp', 'shard')), may hold values from -6 to 6
- velocity: float32 [128, 256, 16], P(('dp', 'shard')), may hold values from -6 to 6
- tstep_idx: int32 [128], P(('dp', 'shard')), may hold values from 0 to 999
- class_ids: int32 [128], P(('dp', 'shard')), may hold values from 0 to 1000
- time_weight: float32 [128], P(('dp', 'shard')), may hold values from 0.3 to 3
- dino: bfloat16 [128, 256, 768], P(('dp', 'shard')), may hold values from -6 to 6
- owner_map: int32 [12], replicated, may hold values from 0 to 11, each once
- adam_flat: float32 [2129920], P(('dp', 'shard')), may hold values from -4 to 4
- adam_m: float32 [2129920], P(('dp', 'shard')), may hold values from -0.015625 to 0.015625
- adam_v: float32 [2129920], P(('dp', 'shard')), may hold values from 1e-06 to 0.0001
- blocks_w: float32 [12, 384, 384], P('shard'), may hold values from -0.3125 to 0.3125
- stat_left: float32 [12, 384, 384], P('shard'), may hold values from -0.005 to 0.01, as said below
- stat_right: float32 [12, 384, 384], P('shard'), may hold values from -0.005 to 0.01, as said below
- root_left: float32 [12, 384, 384], P('shard'), may hold values from -3 to 3, as said below
- root_right: float32 [12, 384, 384], P('shard'), may hold values from -3 to 3, as said below
Outputs:
- loss: float32 [], replicated
- block_update: float32 [12, 384, 384], P('shard')
- stat_left_new: float32 [12, 384, 384], P('shard')
- stat_right_new: float32 [12, 384, 384], P('shard')
- adam_update: float32 [2129920], P(('dp', 'shard'))
- adam_m_new: float32 [2129920], P(('dp', 'shard'))
- adam_v_new: float32 [2129920], P(('dp', 'shard'))
Inputs may be any that keep to these rules, and one draw needn't show every extreme that they name: `owner_map`: each block number appears once. `stat_left`: each slot is symmetric positive definite. `stat_right`: each slot is symmetric positive definite. `root_left`: each slot is symmetric positive definite. `root_right`: each slot is symmetric positive definite.
All inputs are finite; a program needn't handle non-finite values.
Results may differ from a plain program's by a relative error of at most 0.0097.
Values may be sent and summed in bfloat16 or wider, within the bound.
No kernel may reach another device: no remote copies, remote signals or barrier semaphores. Data moves between devices by JAX's collectives and lax.ppermute only.
A program may use at most 192 MiB of HBM per device.

v0:
```python
import functools
import math
import jax
import jax.numpy as jnp
from jax import lax
from jax.sharding import PartitionSpec as P

D = 384
HEADS = 6
HDIM = 64
F = 1536
PD = 16
GRID = 16
SEQ = 256
FREQ = 256
NCLS = 1001
DINO = 768
STEP = 10
NBLK = 12
ADAM_LEN = 2125072
ADAM_PAD = 2129920
HIGHEST = lax.Precision.HIGHEST
BETA_ONE = 0.9
BETA_TWO = 0.95
ADAM_EPS = 1e-08
ADAM_RATE = 0.01
DECAY_RATE = 0.1
STAT_BETA = 0.9
SHAMPOO_RATE = 0.02
RMS_EPS = 1e-08
REPA_WEIGHT = 0.5
NORM_EPS = 1e-06


def segment_shapes():
    return [
        (PD, D),
        (D,),
        (FREQ, D),
        (D,),
        (D, D),
        (D,),
        (NCLS, D),
        (D, 6 * D),
        (6 * D,),
        (D,),
        (D,),
        (D,),
        (F,),
        (D,),
        (D, 2 * D),
        (2 * D,),
        (D, PD),
        (PD,),
        (D, DINO),
        (DINO,),
    ]


def unflatten(flat):
    pieces = []
    offset = 0
    for seg_dims in segment_shapes():
        length = math.prod(seg_dims)
        pieces.append(flat[offset : offset + length].reshape(seg_dims))
        offset += length
    return pieces


def position_table():
    quarter = D // 4
    frequencies = 1.0 / 10000.0 ** (jnp.arange(quarter, dtype=jnp.float32) / quarter)
    cell_ids = jnp.arange(SEQ, dtype=jnp.int32)
    row_arg = (cell_ids // GRID).astype(jnp.float32)[:, None] * frequencies[None, :]
    col_arg = (cell_ids % GRID).astype(jnp.float32)[:, None] * frequencies[None, :]
    return jnp.concatenate(
        [jnp.sin(col_arg), jnp.cos(col_arg), jnp.sin(row_arg), jnp.cos(row_arg)], axis=1
    )


def time_features(tstep_idx):
    half_freq = FREQ // 2
    frequencies = jnp.exp(-math.log(10000.0) * jnp.arange(half_freq, dtype=jnp.float32) / half_freq)
    angles = (tstep_idx.astype(jnp.float32) + 0.5)[:, None] * frequencies[None, :]
    return jnp.concatenate([jnp.cos(angles), jnp.sin(angles)], axis=1)


def normalize(values):
    centered = values - jnp.mean(values, axis=-1, keepdims=True)
    inv_dev = lax.rsqrt(jnp.mean(centered * centered, axis=-1, keepdims=True) + NORM_EPS)
    return (centered * inv_dev, inv_dev)


def normalize_back(grad_in, normed, inv_dev):
    return inv_dev * (
        grad_in
        - jnp.mean(grad_in, axis=-1, keepdims=True)
        - normed * jnp.mean(grad_in * normed, axis=-1, keepdims=True)
    )


def condition_terms(
    tstep_idx,
    class_ids,
    time_in_weight,
    time_in_bias,
    time_out_weight,
    time_out_bias,
    class_table,
    mod_weight,
    mod_bias,
    final_mod_weight,
    final_mod_bias,
):
    features = time_features(tstep_idx)
    time_hidden = jax.nn.silu(jnp.dot(features, time_in_weight, precision=HIGHEST) + time_in_bias)
    onehot_class = (class_ids[:, None] == jnp.arange(NCLS, dtype=jnp.int32)[None, :]).astype(
        jnp.float32
    )
    condition = (
        jnp.dot(time_hidden, time_out_weight, precision=HIGHEST)
        + time_out_bias
        + jnp.dot(onehot_class, class_table, precision=HIGHEST)
    )
    cond_act = jax.nn.silu(condition)
    modulation = jnp.dot(cond_act, mod_weight, precision=HIGHEST) + mod_bias
    final_mods = jnp.dot(cond_act, final_mod_weight, precision=HIGHEST) + final_mod_bias
    return (modulation, final_mods)


def cosine_total(aligned, dino_f):
    products = jnp.sum(aligned * dino_f, axis=-1)
    return jnp.sum(
        products
        * lax.rsqrt(jnp.sum(aligned * aligned, axis=-1) + NORM_EPS)
        * lax.rsqrt(jnp.sum(dino_f * dino_f, axis=-1) + NORM_EPS)
    )


def matmul(left, right):
    return jnp.dot(left, right, preferred_element_type=jnp.float32)


def row_total(rounded):
    return jnp.sum(rounded.astype(jnp.float32), axis=0)


def body(
    noisy,
    velocity,
    tstep_idx,
    class_ids,
    time_weight,
    dino,
    owner_map,
    adam_flat,
    adam_m,
    adam_v,
    blocks_w,
    stat_left,
    stat_right,
    root_left,
    root_right,
):
    devices = lax.axis_size("dp") * lax.axis_size("shard")
    images = noisy.shape[0]
    seq = noisy.shape[1]
    total_img = images * devices
    rows = images * seq
    fc_ratio = F // D
    flat_low = lax.all_gather(adam_flat.astype(jnp.bfloat16), ("dp", "shard"), axis=0, tiled=True)
    slot_low = lax.all_gather(blocks_w.astype(jnp.bfloat16), "shard", axis=0, tiled=True)
    block_ids = jnp.arange(NBLK, dtype=jnp.int32)
    slot_of = jnp.sum(
        block_ids[:, None] * (owner_map[:, None] == block_ids[None, :]).astype(jnp.int32), axis=0
    )
    blocks = jnp.take(slot_low, slot_of, axis=0)
    w_qkv = jnp.concatenate([blocks[0], blocks[1], blocks[2]], axis=1)
    w_proj = blocks[3]
    w_up = jnp.concatenate([blocks[4 + which] for which in range(fc_ratio)], axis=1)
    w_down = blocks[4 + fc_ratio :].reshape(F, D)
    pieces_low = unflatten(flat_low)
    pieces = [piece.astype(jnp.float32) for piece in pieces_low]
    (
        patch_weight,
        patch_bias,
        time_in_weight,
        time_in_bias,
        time_out_weight,
        time_out_bias,
        class_table,
        mod_weight,
        mod_bias,
        query_bias,
        value_bias,
        proj_bias,
        hidden_bias,
        down_bias,
        final_mod_weight,
        final_mod_bias,
        final_weight,
        final_bias,
        align_weight,
        align_bias,
    ) = pieces
    patch_low = pieces_low[0]
    final_low = pieces_low[16]
    align_low = pieces_low[18]
    cond_weights = (
        time_in_weight,
        time_in_bias,
        time_out_weight,
        time_out_bias,
        class_table,
        mod_weight,
        mod_bias,
        final_mod_weight,
        final_mod_bias,
    )
    (modulation, final_mods), cond_back = jax.vjp(
        functools.partial(condition_terms, tstep_idx, class_ids), *cond_weights
    )
    shift_one, scale_one, gate_one, shift_two, scale_two, gate_two = [
        modulation[:, None, which * D : (which + 1) * D] for which in range(6)
    ]
    final_shift = final_mods[:, None, :D]
    final_scale = final_mods[:, None, D:]
    noisy_low = noisy.astype(jnp.bfloat16).reshape(rows, PD)
    hidden0 = (matmul(noisy_low, patch_low) + patch_bias).reshape(images, seq, D) + position_table()
    norm_one, inv_one = normalize(hidden0)
    act_one = (norm_one * (1.0 + scale_one) + shift_one).astype(jnp.bfloat16).reshape(rows, D)
    qkv_bias = jnp.concatenate([query_bias, jnp.zeros((D,), jnp.float32), value_bias])
    projected = (
        (matmul(act_one, w_qkv) + qkv_bias)
        .astype(jnp.bfloat16)
        .reshape(images, seq, 3, HEADS, HDIM)
    )
    queries = projected[:, :, 0]
    key_part = projected[:, :, 1]
    values = projected[:, :, 2]
    scale_qk = HDIM ** (-0.5)
    scores = (
        jnp.einsum("gqhe,gkhe->ghqk", queries, key_part, preferred_element_type=jnp.float32)
        * scale_qk
    )
    row_max = jnp.max(scores, axis=-1, keepdims=True)
    log_total = row_max + jnp.log(jnp.sum(jnp.exp(scores - row_max), axis=-1, keepdims=True))
    probs_low = jnp.exp(scores - log_total).astype(jnp.bfloat16)
    attended = (
        jnp.einsum("ghqk,gkhe->gqhe", probs_low, values, preferred_element_type=jnp.float32)
        .reshape(rows, D)
        .astype(jnp.bfloat16)
    )
    branch_one = (matmul(attended, w_proj) + proj_bias).reshape(images, seq, D)
    hidden1 = hidden0 + gate_one * branch_one
    norm_two, inv_two = normalize(hidden1)
    act_two = (norm_two * (1.0 + scale_two) + shift_two).astype(jnp.bfloat16).reshape(rows, D)
    inner_pre = matmul(act_two, w_up) + hidden_bias
    gelu_out, gelu_back = jax.vjp(functools.partial(jax.nn.gelu, approximate=True), inner_pre)
    gelu_low = gelu_out.astype(jnp.bfloat16)
    branch_two = (matmul(gelu_low, w_down) + down_bias).reshape(images, seq, D)
    hidden2 = hidden1 + gate_two * branch_two
    norm_three, inv_three = normalize(hidden2)
    act_three = (
        (norm_three * (1.0 + final_scale) + final_shift).astype(jnp.bfloat16).reshape(rows, D)
    )
    output = (matmul(act_three, final_low) + final_bias).reshape(images, seq, PD)
    errors = output - velocity
    main_term = jnp.sum(time_weight[:, None, None] * errors * errors) / (total_img * SEQ * PD)
    hidden1_low = hidden1.astype(jnp.bfloat16).reshape(rows, D)
    aligned = matmul(hidden1_low, align_low) + align_bias
    dino_f = dino.astype(jnp.float32).reshape(rows, DINO)
    cosine_sum, cosine_back = jax.vjp(functools.partial(cosine_total, dino_f=dino_f), aligned)
    align_scale = REPA_WEIGHT / (total_img * SEQ)
    loss_local = main_term - align_scale * cosine_sum
    back_output = (
        (2.0 * time_weight[:, None, None] * errors / (total_img * SEQ * PD))
        .reshape(rows, PD)
        .astype(jnp.bfloat16)
    )
    grad_final = matmul(act_three.T, back_output)
    grad_final_bias = row_total(back_output)
    back_three = matmul(back_output, final_low.T).reshape(images, seq, D)
    grad_final_shift = jnp.sum(back_three, axis=1)
    grad_final_scale = jnp.sum(back_three * norm_three, axis=1)
    back_hidden2 = normalize_back(back_three * (1.0 + final_scale), norm_three, inv_three)
    back_branch_two = (back_hidden2 * gate_two).reshape(rows, D).astype(jnp.bfloat16)
    grad_gate_two = jnp.sum(back_hidden2 * branch_two, axis=1)
    grad_down = matmul(gelu_low.T, back_branch_two)
    grad_down_bias = row_total(back_branch_two)
    back_inner = gelu_back(matmul(back_branch_two, w_down.T))[0].astype(jnp.bfloat16)
    grad_up = matmul(act_two.T, back_inner)
    grad_hidden_bias = row_total(back_inner)
    back_two = matmul(back_inner, w_up.T).reshape(images, seq, D)
    grad_shift_two = jnp.sum(back_two, axis=1)
    grad_scale_two = jnp.sum(back_two * norm_two, axis=1)
    back_aligned = cosine_back(jnp.asarray(-align_scale, jnp.float32))[0].astype(jnp.bfloat16)
    grad_align = matmul(hidden1_low.T, back_aligned)
    grad_align_bias = row_total(back_aligned)
    back_hidden1 = (
        back_hidden2
        + normalize_back(back_two * (1.0 + scale_two), norm_two, inv_two)
        + matmul(back_aligned, align_low.T).reshape(images, seq, D)
    )
    back_branch_one = (back_hidden1 * gate_one).reshape(rows, D).astype(jnp.bfloat16)
    grad_gate_one = jnp.sum(back_hidden1 * branch_one, axis=1)
    grad_proj = matmul(attended.T, back_branch_one)
    grad_proj_bias = row_total(back_branch_one)
    back_attended = (
        matmul(back_branch_one, w_proj.T).astype(jnp.bfloat16).reshape(images, seq, HEADS, HDIM)
    )
    back_probs = jnp.einsum(
        "gqhe,gkhe->ghqk", back_attended, values, preferred_element_type=jnp.float32
    )
    grad_values = jnp.einsum(
        "ghqk,gqhe->gkhe", probs_low, back_attended, preferred_element_type=jnp.float32
    )
    scores_again = (
        jnp.einsum("gqhe,gkhe->ghqk", queries, key_part, preferred_element_type=jnp.float32)
        * scale_qk
    )
    probs_again = jnp.exp(scores_again - log_total)
    back_scores = (
        probs_again * (back_probs - jnp.sum(back_probs * probs_again, axis=-1, keepdims=True))
    ).astype(jnp.bfloat16)
    grad_queries = (
        jnp.einsum("ghqk,gkhe->gqhe", back_scores, key_part, preferred_element_type=jnp.float32)
        * scale_qk
    )
    grad_keys = (
        jnp.einsum("ghqk,gqhe->gkhe", back_scores, queries, preferred_element_type=jnp.float32)
        * scale_qk
    )
    back_projected = (
        jnp.stack([grad_queries, grad_keys, grad_values], axis=2)
        .reshape(rows, 3 * D)
        .astype(jnp.bfloat16)
    )
    grad_qkv = matmul(act_one.T, back_projected)
    grad_qkv_bias = row_total(back_projected)
    back_one = matmul(back_projected, w_qkv.T).reshape(images, seq, D)
    grad_shift_one = jnp.sum(back_one, axis=1)
    grad_scale_one = jnp.sum(back_one * norm_one, axis=1)
    back_hidden0 = (
        (back_hidden1 + normalize_back(back_one * (1.0 + scale_one), norm_one, inv_one))
        .reshape(rows, D)
        .astype(jnp.bfloat16)
    )
    grad_patch = matmul(noisy_low.T, back_hidden0)
    grad_patch_bias = row_total(back_hidden0)
    grad_modulation = jnp.concatenate(
        [
            grad_shift_one,
            grad_scale_one,
            grad_gate_one,
            grad_shift_two,
            grad_scale_two,
            grad_gate_two,
        ],
        axis=1,
    )
    grad_final_mods = jnp.concatenate([grad_final_shift, grad_final_scale], axis=1)
    cond_grads = cond_back((grad_modulation, grad_final_mods))
    grad_list = (
        [grad_patch, grad_patch_bias]
        + list(cond_grads[:7])
        + [
            grad_qkv_bias[:D],
            grad_qkv_bias[2 * D :],
            grad_proj_bias,
            grad_hidden_bias,
            grad_down_bias,
            cond_grads[7],
            cond_grads[8],
            grad_final,
            grad_final_bias,
            grad_align,
            grad_align_bias,
        ]
    )
    flat_grad = jnp.concatenate(
        [gradient_part.reshape(-1) for gradient_part in grad_list]
        + [jnp.zeros((ADAM_PAD - ADAM_LEN,), jnp.float32)]
    )
    grad_model = jnp.concatenate(
        [
            grad_qkv.reshape(D, 3, D).transpose(1, 0, 2),
            grad_proj[None],
            grad_up.reshape(D, fc_ratio, D).transpose(1, 0, 2),
            grad_down.reshape(fc_ratio, D, D),
        ],
        axis=0,
    )
    grad_slot = jnp.take(grad_model, owner_map, axis=0)
    flat_owned = lax.psum_scatter(flat_grad, ("dp", "shard"), scatter_dimension=0, tiled=True)
    loss_total = lax.psum(loss_local, ("dp", "shard"))
    summed = lax.psum(grad_slot, "dp")
    owned = lax.psum_scatter(
        summed.astype(jnp.bfloat16), "shard", scatter_dimension=0, tiled=True
    ).astype(jnp.float32)
    new_left = STAT_BETA * stat_left + (1.0 - STAT_BETA) * jnp.einsum(
        "bij,bkj->bik", owned, owned, precision=HIGHEST
    )
    new_right = STAT_BETA * stat_right + (1.0 - STAT_BETA) * jnp.einsum(
        "bji,bjk->bik", owned, owned, precision=HIGHEST
    )
    left_applied = jnp.einsum("bij,bjk->bik", root_left, owned, precision=HIGHEST)
    direction = jnp.einsum("bij,bjk->bik", left_applied, root_right, precision=HIGHEST)
    root_mean = jnp.sqrt(jnp.mean(direction * direction, axis=(1, 2), keepdims=True))
    block_update = -SHAMPOO_RATE * (direction / (root_mean + RMS_EPS) + DECAY_RATE * blocks_w)
    new_m = BETA_ONE * adam_m + (1.0 - BETA_ONE) * flat_owned
    new_v = BETA_TWO * adam_v + (1.0 - BETA_TWO) * flat_owned * flat_owned
    corrected_m = new_m / (1.0 - BETA_ONE**STEP)
    corrected_v = new_v / (1.0 - BETA_TWO**STEP)
    adam_update = -ADAM_RATE * (
        corrected_m / (jnp.sqrt(corrected_v) + ADAM_EPS) + DECAY_RATE * adam_flat
    )
    return (loss_total, block_update, new_left, new_right, adam_update, new_m, new_v)


def solution(mesh):
    return jax.shard_map(
        body,
        mesh=mesh,
        in_specs=(
            P(("dp", "shard"), None, None),
            P(("dp", "shard"), None, None),
            P(("dp", "shard")),
            P(("dp", "shard")),
            P(("dp", "shard")),
            P(("dp", "shard"), None, None),
            P(),
            P(("dp", "shard")),
            P(("dp", "shard")),
            P(("dp", "shard")),
            P("shard", None, None),
            P("shard", None, None),
            P("shard", None, None),
            P("shard", None, None),
            P("shard", None, None),
        ),
        out_specs=(
            P(),
            P("shard", None, None),
            P("shard", None, None),
            P("shard", None, None),
            P(("dp", "shard")),
            P(("dp", "shard")),
            P(("dp", "shard")),
        ),
        check_vma=False,
    )
```

profile of v0, /device:TPU:0, one launch (start us, length us, event | category | flops | bytes accessed | tf_op | source)
XLA Modules:
  0.0 797.5 jit_solution(3456417252762726016)
XLA Ops:
  17.3 26.3 %all-gather.5.cloned.1.call-done = bf16[12,384,384]{2,1,0:T(8,128)(2,1)} async-done(((bf16[3,384,384]{2,1,0:T(8,128)(2,1)}), bf16[12,384,384]{2,1,0:T(8,128)(2,1)}) %all-gather.5.cloned.1.call-update) | async-done | bytes 3538960 | tf_op jit(solution)/shard_map/all_gather | solution.py:172
  43.6 5.1 gather_fusion
  54.7 54.4 %all-gather.3.cloned.1.call-done = bf16[2129920]{0:T(1024)(128)(2,1)} async-done(((bf16[66560]{0:T(1024)(128)(2,1)}), bf16[2129920]{0:T(1024)(128)(2,1)}) %all-gather.3.cloned.1.call-update) | async-done | bytes 4259856 | tf_op jit(solution)/shard_map/all_gather | solution.py:171
  140.5 4.3 copy.90
  144.9 6.1 reshape.436
  159.4 3.6 fusion.106
  169.8 3.8 fusion.104
  188.0 7.3 fusion.13
  195.3 5.1 convert_reduce_fusion
  203.7 3.5 multiply_reduce_fusion.2
  221.7 7.7 multiply_reduce_fusion
  229.4 6.3 multiply_convert_fusion
  252.4 4.8 fusion.95
  276.5 4.7 reshape.451
  300.5 87.2 %concatenate.35 = f32[2129920]{0:T(1024)} concatenate(f32[6144]{0:T(1024)} %reshape.447, f32[384]{0:T(512)} %get-tuple-element.39, f32[98304]{0:T(1024)S(1)} %copy-done.57, f32[384]{0:T(512)} %get-tuple-element.37, f32[147456]{0:T(1024)S(1)} %reshape.449, f32[384]{0:T(512)} %get-tuple-element.110, f32[384384]{0:T(1024)} %reshape.450, f32[884736]{0:T(1024)} %reshape.451, ...), dimensions={0} | concatenate | bytes 17039360 | tf_op jit(solution)/shard_map/concatenate | solution.py:381
  391.3 4.9 copy.131
  396.2 5.1 convolution_bitcast_fusion
  401.3 4.7 copy.132
  406.1 4.2 fusion.114
  413.5 7.0 gather_fusion.1
  420.6 6.6 broadcast_select_fusion
  427.1 306.0 %all-reduce.5 = bf16[12,384,384]{2,1,0:T(8,128)(2,1)} all-reduce(f32[12,384,384]{2,1,0:T(8,128)} %broadcast_select_fusion), channel_id=1, replica_groups=mesh['dp'=8,'shard'=4] {'dp'}, use_global_device_ids=true, to_apply=%region_20.21 | all-reduce | flops 1769472 | bytes 10616832 | tf_op jit(solution)/shard_map/psum | solution.py:397
  734.7 40.7 %psum.14 = f32[]{:T(128)} all-reduce(f32[]{:T(128)S(6)} %sub.143), channel_id=1, replica_groups=mesh['dp'=8,'shard'=4] {'dp','shard'}, use_global_device_ids=true, to_apply=%region_14.15 | all-reduce | flops 1 | bytes 8 | tf_op jit(solution)/shard_map/psum | solution.py:396
  780.6 3.8 multiply_reduce_fusion.3
  (368 shorter events, 167.8 us)
Async XLA Ops:
  7.2 773.4 %copy-start = (f32[3,384,384]{2,1,0:T(8,128)S(1)}, f32[3,384,384]{2,1,0:T(8,128)}, u32[]{:S(2)}) copy-start(f32[3,384,384]{2,1,0:T(8,128)} %param.29) | copy-start | bytes 5308420
  7.2 36.4 %all-gather.5.cloned.1.call-start = ((), (), s32[]{:S(2)}) async-start(), calls=%async_computation.2 | async-start | bytes 4423680 | tf_op jit(solution)/shard_map/all_gather | solution.py:172
  9.9 99.2 %all-gather.3.cloned.1.call-start = ((), (), s32[]{:S(2)}) async-start(), calls=%async_computation.1 | async-start | bytes 4392960 | tf_op jit(solution)/shard_map/all_gather | solution.py:171
  11.6 763.7 %all-reduce.4.cloned.1.call-start = ((), (), s32[]{:S(2)}) async-start(), calls=%async_computation.4 | async-start | bytes 17039360
  17.3 114.4 %copy-start.88 = (f32[4,128]{1,0:T(4,128)}, f32[4,128]{1,0:T(4,128)S(1)}, u32[]{:S(2)}) copy-start(f32[4,128]{1,0:T(4,128)S(1)} %get-tuple-element.90) | copy-start | bytes 6148
  17.3 114.4 %copy-start.90 = (f32[4,128]{1,0:T(4,128)}, f32[4,128]{1,0:T(4,128)S(1)}, u32[]{:S(2)}) copy-start(f32[4,128]{1,0:T(4,128)S(1)} %get-tuple-element.91) | copy-start | bytes 6148
  169.8 6.8 copy-start.82
  180.8 7.1 slice-start.2
  182.8 5.2 slice-start.3
  188.0 7.3 copy-start.66
  195.3 5.1 copy-start.59
  221.7 17.5 %slice-start = ((s8[6291456]{0:T(1024)(128)(4,1)}), s8[4194304]{0:T(1024)(128)(4,1)S(1)}, s32[]{:S(2)}) async-start(s8[6291456]{0:T(1024)(128)(4,1)} %bitcast.283), calls=%async_computation.5 | async-start | bytes 8388608
  229.4 6.4 copy-start.26
  229.4 9.8 %slice-start.1 = ((s8[6291456]{0:T(1024)(128)(4,1)}), s8[2097152]{0:T(1024)(128)(4,1)S(1)}, s32[]{:S(2)}) async-start(s8[6291456]{0:T(1024)(128)(4,1)} %bitcast.283), calls=%async_computation.6 | async-start | bytes 4194304
  252.4 5.3 copy-start.18
  257.7 6.1 copy-start.50
  257.7 7.7 copy-start.4
  265.5 6.2 copy-start.16
  282.4 8.4 %copy-start.38 = (f32[384,768]{1,0:T(8,128)S(1)}, f32[384,768]{1,0:T(8,128)}, u32[]{:S(2)}) copy-start(f32[384,768]{1,0:T(8,128)} %fusion.46) | copy-start | bytes 3538948
  291.9 6.4 copy-start.33
  291.9 8.6 %copy-start.57 = (f32[98304]{0:T(1024)S(1)}, f32[98304]{0:T(1024)}, u32[]{:S(2)}) copy-start(f32[98304]{0:T(1024)} %reshape.448) | copy-start | bytes 1179652
  387.7 389.8 %reduce-scatter.2.cloned.1.call-start = ((), (), s32[]{:S(2)}) async-start(), calls=%async_computation.3 | async-start | bytes 4423680 | tf_op jit(solution)/shard_map/reduce_scatter | solution.py:398
  413.5 7.0 copy-start.95
  733.2 44.4 %copy-start.54 = (f32[3,384,384]{2,1,0:T(8,128)S(1)}, f32[3,384,384]{2,1,0:T(8,128)}, u32[]{:S(2)}) copy-start(f32[3,384,384]{2,1,0:T(8,128)} %param.28) | copy-start | bytes 5308420
  (83 other events, 246.4 us)
Sparse Core Ops, SparseCore 0:
  10.1 33.4 all-gather.4
  47.1 61.9 all-gather.2
  387.8 243.0 all-reduce.3
  733.3 39.5 reduce-scatter.1
where the time goes:
time: 810 us; the launch traced here: 798 us
  blocking collectives  347 us (43%)
  local copies, waits for them, and re-layouts  186 us (23%)
  matrix products  103 us (13%)
  waiting for transfers between devices  80.8 us (10%)
  other arithmetic  64.9 us (8%)
  between operations  16.6 us (2%)
    psum x1, blocking collectives, body(): summed = lax.psum(grad_slot, 'dp')  306 us
    concatenate x1, local copies, waits for them, and re-layouts, body(): jnp.concatenate([gradient_part.reshape(-1) for gradient_part in grad_list...  87.2 us
    dot_general x20, matrix products, matmul(): return jnp.dot(left, right, preferred_element_type=jnp.float32)  57.1 us
    all_gather x1, waiting for transfers between devices, body(): lax.all_gather(adam_flat.astype(jnp.bfloat16), ('dp', 'shard'), axis=0, t...  54.4 us
    psum x1, blocking collectives, body(): loss_total = lax.psum(loss_local, ('dp', 'shard'))  40.7 us
    all_gather x1, waiting for transfers between devices, body(): lax.all_gather(blocks_w.astype(jnp.bfloat16), 'shard', axis=0, tiled=True)  26.3 us
  transfers between devices with their start and end apart: 4, of which 2 were waited for; matrix products, arithmetic and copies ran while one was open for 7% of the time, Pallas kernels for 0%

commit v1 on v0

--- a/solution.py
+++ b/solution.py
@@ -394,7 +394,9 @@
     grad_slot = jnp.take(grad_model, owner_map, axis=0)
     flat_owned = lax.psum_scatter(flat_grad, ("dp", "shard"), scatter_dimension=0, tiled=True)
     loss_total = lax.psum(loss_local, ("dp", "shard"))
-    summed = lax.psum(grad_slot, "dp")
+    summed = grad_slot
+    for hop in (1, 2, 4):
+        summed = summed + lax.ppermute(summed, "dp", [(dev, dev ^ hop) for dev in range(8)])
     owned = lax.psum_scatter(
         summed.astype(jnp.bfloat16), "shard", scatter_dimension=0, tiled=True
     ).astype(jnp.float32)

time: 810 us -> 1140 us (1.41)
  waiting for transfers between devices: 80.8 us -> 702 us
  blocking collectives: 347 us -> 37.2 us
  other arithmetic: 64.9 us -> 80.5 us
    ppermute x0 -> x3, waiting for transfers between devices: none -> 516 us  [body(): lax.ppermute(summed, 'dp', [(dev, dev ^ hop) for dev in range(8)])]
    psum x1 -> x0, blocking collectives: 306 us -> none  [body(): summed = lax.psum(grad_slot, 'dp')]
    unnamed x5, waiting for transfers between devices: 0.07 us -> 64.4 us
    reduce_scatter x1, waiting for transfers between devices: 0.01 us -> 40.7 us  [body(): lax.psum_scatter(summed.astype(jnp.bfloat16), 'shard', scatter_dimension=...]
    add x0 -> x2, other arithmetic: none -> 13.2 us  [body(): summed + lax.ppermute(summed, 'dp', [(dev, dev ^ hop) for dev in range(8)])]
  transfers between devices with their start and end apart: 4 -> 7, of which waited for: 2 -> 7; matrix products, arithmetic and copies ran while one was open for 7% -> 15% of each run, Pallas kernels for 0% -> 0%
where the time goes in v1:
time: 1140 us; the launch traced here: 1130 us
  waiting for transfers between devices  702 us (62%)
  local copies, waits for them, and re-layouts  185 us (16%)
  matrix products  103 us (9%)
  other arithmetic  80.5 us (7%)
  blocking collectives  37.2 us (3%)
  between operations  16.8 us (1%)
    ppermute x3, waiting for transfers between devices, body(): lax.ppermute(summed, 'dp', [(dev, dev ^ hop) for dev in range(8)])  516 us
    concatenate x1, local copies, waits for them, and re-layouts, body(): jnp.concatenate([gradient_part.reshape(-1) for gradient_part in grad_list...  87.1 us
    unnamed x5, waiting for transfers between devices  64.4 us
    dot_general x20, matrix products, matmul(): return jnp.dot(left, right, preferred_element_type=jnp.float32)  59.6 us
    all_gather x1, waiting for transfers between devices, body(): lax.all_gather(adam_flat.astype(jnp.bfloat16), ('dp', 'shard'), axis=0, t...  54.3 us
    reduce_scatter x1, waiting for transfers between devices, body(): lax.psum_scatter(summed.astype(jnp.bfloat16), 'shard', scatter_dimension=...  40.7 us
    psum x1, blocking collectives, body(): loss_total = lax.psum(loss_local, ('dp', 'shard'))  37.2 us
    all_gather x1, waiting for transfers between devices, body(): lax.all_gather(blocks_w.astype(jnp.bfloat16), 'shard', axis=0, tiled=True)  26.3 us
  transfers between devices with their start and end apart: 7, of which 7 were waited for; matrix products, arithmetic and copies ran while one was open for 15% of the time, Pallas kernels for 0%

profile of v1, /device:TPU:0, one launch (start us, length us, event | category | flops | bytes accessed | tf_op | source)
XLA Modules:
  0.0 1129.1 jit_solution(8352932541695347337)
XLA Ops:
  17.3 26.3 %all-gather.5.cloned.1.call-done = bf16[12,384,384]{2,1,0:T(8,128)(2,1)} async-done(((bf16[3,384,384]{2,1,0:T(8,128)(2,1)}), bf16[12,384,384]{2,1,0:T(8,128)(2,1)}) %all-gather.5.cloned.1.call-update) | async-done | bytes 3538960 | tf_op jit(solution)/shard_map/all_gather | solution.py:172
  43.6 5.1 gather_fusion
  54.8 54.3 %all-gather.3.cloned.1.call-done = bf16[2129920]{0:T(1024)(128)(2,1)} async-done(((bf16[66560]{0:T(1024)(128)(2,1)}), bf16[2129920]{0:T(1024)(128)(2,1)}) %all-gather.3.cloned.1.call-update) | async-done | bytes 4259856 | tf_op jit(solution)/shard_map/all_gather | solution.py:171
  144.9 6.1 reshape.436
  186.2 7.4 fusion.13
  193.6 5.1 convert_reduce_fusion
  220.6 7.5 multiply_reduce_fusion
  228.1 6.5 multiply_convert_fusion
  246.3 5.0 copy.131
  251.3 5.0 convolution_bitcast_fusion
  256.3 4.6 copy.132
  268.2 7.0 gather_fusion.1
  280.5 153.2 %collective-permute-done = f32[12,384,384]{2,1,0:T(8,128)} collective-permute-done((f32[12,384,384]{2,1,0:T(8,128)S(1)}, f32[12,384,384]{2,1,0:T(8,128)}, u32[]{:S(2)}, u32[]{:S(2)}) %collective-permute-start) | collective-permute-done | bytes 7077920 | tf_op jit(solution)/shard_map/ppermute | solution.py:399
  433.7 6.7 fusion.168
  451.0 143.3 %collective-permute-done.1 = f32[12,384,384]{2,1,0:T(8,128)} collective-permute-done((f32[12,384,384]{2,1,0:T(8,128)}, f32[12,384,384]{2,1,0:T(8,128)}, u32[]{:S(2)}, u32[]{:S(2)}) %collective-permute-start.1) | collective-permute-done | bytes 7077920 | tf_op jit(solution)/shard_map/ppermute | solution.py:399
  594.3 6.5 add.422
  603.3 4.8 fusion.95
  608.2 4.8 reshape.451
  648.5 87.1 %concatenate.35 = f32[2129920]{0:T(1024)} concatenate(f32[6144]{0:T(1024)} %reshape.447, f32[384]{0:T(512)} %get-tuple-element.39, f32[98304]{0:T(1024)S(1)} %copy-done.56, f32[384]{0:T(512)} %get-tuple-element.37, f32[147456]{0:T(1024)S(1)} %copy-done.49, f32[384]{0:T(512)} %get-tuple-element.110, f32[384384]{0:T(1024)} %reshape.450, f32[884736]{0:T(1024)} %reshape.451, ...), dimensions={0} | concatenate | bytes 17039360 | tf_op jit(solution)/shard_map/concatenate | solution.py:381
  735.9 219.5 %collective-permute-done.2 = f32[12,384,384]{2,1,0:T(8,128)} collective-permute-done((f32[12,384,384]{2,1,0:T(8,128)}, f32[12,384,384]{2,1,0:T(8,128)}, u32[]{:S(2)}, u32[]{:S(2)}) %collective-permute-start.2) | collective-permute-done | bytes 7077920 | tf_op jit(solution)/shard_map/ppermute | solution.py:399
  955.4 7.7 add_convert_fusion
  964.6 37.2 %psum.7 = f32[]{:T(128)} all-reduce(f32[]{:T(128)S(6)} %sub.143), channel_id=1, replica_groups=mesh['dp'=8,'shard'=4] {'dp','shard'}, use_global_device_ids=true, to_apply=%region_14.15 | all-reduce | flops 1 | bytes 8 | tf_op jit(solution)/shard_map/psum | solution.py:396
  1001.9 64.4 %all-reduce.3.cloned.1.call-done = f32[2129920]{0:T(1024)} async-done(((f32[2129920]{0:T(1024)}), f32[2129920]{0:T(1024)}) %all-reduce.3.cloned.1.call-update) | async-done | bytes 8519696
  1068.4 40.7 %reduce-scatter.2.cloned.1.call-done = bf16[3,384,384]{2,1,0:T(8,128)(2,1)} async-done(((bf16[12,384,384]{2,1,0:T(8,128)(2,1)}), bf16[3,384,384]{2,1,0:T(8,128)(2,1)}) %reduce-scatter.2.cloned.1.call-update) | async-done | bytes 884752 | tf_op jit(solution)/shard_map/reduce_scatter | solution.py:400
  (395 shorter events, 196.4 us)
Async XLA Ops:
  7.2 1105.0 %copy-start = (f32[3,384,384]{2,1,0:T(8,128)S(1)}, f32[3,384,384]{2,1,0:T(8,128)}, u32[]{:S(2)}) copy-start(f32[3,384,384]{2,1,0:T(8,128)} %param.29) | copy-start | bytes 5308420
  7.2 36.4 %all-gather.5.cloned.1.call-start = ((), (), s32[]{:S(2)}) async-start(), calls=%async_computation.2 | async-start | bytes 4423680 | tf_op jit(solution)/shard_map/all_gather | solution.py:172
  9.9 99.2 %all-gather.3.cloned.1.call-start = ((), (), s32[]{:S(2)}) async-start(), calls=%async_computation.1 | async-start | bytes 4392960 | tf_op jit(solution)/shard_map/all_gather | solution.py:171
  11.6 1054.6 %all-reduce.3.cloned.1.call-start = ((), (), s32[]{:S(2)}) async-start(), calls=%async_computation.4 | async-start | bytes 17039360
  17.3 114.3 %copy-start.94 = (f32[4,128]{1,0:T(4,128)}, f32[4,128]{1,0:T(4,128)S(1)}, u32[]{:S(2)}) copy-start(f32[4,128]{1,0:T(4,128)S(1)} %get-tuple-element.90) | copy-start | bytes 6148
  17.3 114.3 %copy-start.96 = (f32[4,128]{1,0:T(4,128)}, f32[4,128]{1,0:T(4,128)S(1)}, u32[]{:S(2)}) copy-start(f32[4,128]{1,0:T(4,128)S(1)} %get-tuple-element.91) | copy-start | bytes 6148
  136.3 28.6 %copy-start.83 = (f32[4,384]{1,0:T(4,128)}, f32[4,384]{1,0:T(4,128)S(1)}, u32[]{:S(2)}) copy-start(f32[4,384]{1,0:T(4,128)S(1)} %get-tuple-element.117) | copy-start | bytes 18436
  164.8 42.6 %copy-start.89 = (f32[4,256]{1,0:T(4,128)}, f32[4,256]{1,0:T(4,128)S(1)}, u32[]{:S(2)}) copy-start(f32[4,256]{1,0:T(4,128)S(1)} %rsqrt.60) | copy-start | bytes 12292
  220.6 16.3 %slice-start = ((s8[6291456]{0:T(1024)(128)(4,1)}), s8[4194304]{0:T(1024)(128)(4,1)S(1)}, s32[]{:S(2)}) async-start(s8[6291456]{0:T(1024)(128)(4,1)} %bitcast.283), calls=%async_computation.5 | async-start | bytes 8388608
  275.2 158.5 %copy-start.5 = (f32[12,384,384]{2,1,0:T(8,128)S(1)}, f32[12,384,384]{2,1,0:T(8,128)}, u32[]{:S(2)}) copy-start(f32[12,384,384]{2,1,0:T(8,128)} %gather_fusion.1) | copy-start | bytes 21233668
  279.0 162.7 %copy-start.17 = (bf16[4,256,3,6,64]{1,4,3,0,2:T(8,128)(2,1)S(1)}, bf16[4,256,3,6,64]{1,4,3,0,2:T(8,128)(2,1)}, u32[]{:S(2)}) copy-start(bf16[4,256,3,6,64]{1,4,3,0,2:T(8,128)(2,1)} %copy-done.16) | copy-start | bytes 7077892
  279.0 154.7 %collective-permute-start = (f32[12,384,384]{2,1,0:T(8,128)S(1)}, f32[12,384,384]{2,1,0:T(8,128)}, u32[]{:S(2)}, u32[]{:S(2)}) collective-permute-start(f32[12,384,384]{2,1,0:T(8,128)S(1)} %broadcast_select_fusion), channel_id=1, source_target_pairs={{0,4},{4,0},{8,12},{12,8},{16,20},{20,16},{24,28},{28,24},{1,5},{5... | collective-permute-start | bytes 21233672 | tf_op jit(solution)/shard_map/ppermute | solution.py:399
  440.3 154.0 %collective-permute-start.1 = (f32[12,384,384]{2,1,0:T(8,128)}, f32[12,384,384]{2,1,0:T(8,128)}, u32[]{:S(2)}, u32[]{:S(2)}) collective-permute-start(f32[12,384,384]{2,1,0:T(8,128)} %fusion.168), channel_id=1, source_target_pairs={{0,8},{4,12},{8,0},{12,4},{16,24},{20,28},{24,16},{28,20},{1,9},{5... | collective-permute-start | bytes 21233672 | tf_op jit(solution)/shard_map/ppermute | solution.py:399
  443.3 151.0 %slice-start.2 = ((s8[7077888]{0:T(1024)(128)(4,1)}), s8[4194304]{0:T(1024)(128)(4,1)S(1)}, s32[]{:S(2)}) async-start(s8[7077888]{0:T(1024)(128)(4,1)} %bitcast.288), calls=%async_computation.7 | async-start | bytes 8388608
  447.9 146.4 %slice-start.3 = ((s8[7077888]{0:T(1024)(128)(4,1)}), s8[2883584]{0:T(1024)(128)(4,1)S(1)}, s32[]{:S(2)}) async-start(s8[7077888]{0:T(1024)(128)(4,1)} %bitcast.288), calls=%async_computation.8 | async-start | bytes 5767168
  451.0 151.5 %copy-start.21 = (f32[1024,384]{1,0:T(8,128)S(1)}, f32[1024,384]{1,0:T(8,128)}, u32[]{:S(2)}) copy-start(f32[1024,384]{1,0:T(8,128)} %get-tuple-element.99) | copy-start | bytes 4718596
  451.0 151.5 %copy-start.23 = (f32[4,256,384]{2,1,0:T(8,128)S(1)}, f32[4,256,384]{2,1,0:T(8,128)}, u32[]{:S(2)}) copy-start(f32[4,256,384]{2,1,0:T(8,128)} %get-tuple-element.30) | copy-start | bytes 4718596
  600.9 354.6 %collective-permute-start.2 = (f32[12,384,384]{2,1,0:T(8,128)}, f32[12,384,384]{2,1,0:T(8,128)}, u32[]{:S(2)}, u32[]{:S(2)}) collective-permute-start(f32[12,384,384]{2,1,0:T(8,128)} %add.422), channel_id=1, source_target_pairs={{0,16},{4,20},{8,24},{12,28},{16,0},{20,4},{24,8},{28,12},{1,17},{... | collective-permute-start | bytes 21233672 | tf_op jit(solution)/shard_map/ppermute | solution.py:399
  637.0 9.3 copy-start.35
  639.2 9.3 copy-start.78
  639.2 9.3 copy-start.49
  639.2 9.3 copy-start.56
  735.7 373.5 %reduce-scatter.2.cloned.1.call-start = ((), (), s32[]{:S(2)}) async-start(), calls=%async_computation.3 | async-start | bytes 4423680 | tf_op jit(solution)/shard_map/reduce_scatter | solution.py:400
  963.2 146.0 %copy-start.52 = (f32[3,384,384]{2,1,0:T(8,128)S(1)}, f32[3,384,384]{2,1,0:T(8,128)}, u32[]{:S(2)}) copy-start(f32[3,384,384]{2,1,0:T(8,128)} %param.28) | copy-start | bytes 5308420
  (95 other events, 338.0 us)
Sparse Core Ops, SparseCore 0:
  10.1 33.4 all-gather.4
  47.1 61.9 all-gather.2
  735.8 330.4 all-reduce.2
  1068.7 40.4 reduce-scatter.1
